TPU v7x, 32 devices: a whole 2x2x4 slice. The times are simulated.
32 devices in a mesh: pts: 8 (over z, y), feat: 4 (over x, core).
Axes of the slice: x: 2, y: 2, z: 4, core: 2. Of those that a mesh axis runs over, the one named last changes fastest.
Arguments:
- slab: bfloat16 [16384, 768], P('pts', 'feat'), may hold values from -40 to 40
- centres: bfloat16 [4096, 768], replicated, may hold values from -3 to 3
- labels: int32 [16384, 1], P(('pts', 'feat')), may hold values from 0 to 4095
- sample_rows: int32 [8, 8, 4], P('pts'), may hold values from 0 to 2047, as said below
- sample_count: int32 [8, 8], P('pts'), may hold values from 0 to 4, as said below
- slot_offset: int32 [8, 8], P('pts'), may hold values from 0 to 28, as said below
Outputs:
- coreset: bfloat16 [256, 768], P('pts', 'feat')
Inputs may be any that keep to these rules, and one draw needn't show every extreme that they name: `sample_rows`: row indices within a source shard; sampled independently with replacement. `sample_count`: in every draw some owner receives 4 rows from every source. slot_offset[o,p] is the sum of sample_count[q,o] over sources q < p.
All inputs are finite; a program needn't handle non-finite values.
Results may differ from a plain program's by a relative error of at most 0.0006.
Values may be sent and summed in bfloat16 or wider, within the bound.
A program may use at most 64 MiB of HBM per device.

v0:
```python
import jax
import jax.numpy as jnp
from jax import lax
from jax.sharding import PartitionSpec as P


def local(slab, centres, labels, sample_rows, sample_count, slot_offset):
    rows_pts, feat_width = slab.shape
    feat_count = lax.axis_size("feat")
    rows_dev = rows_pts // feat_count
    centre_count = centres.shape[0]
    contract = (((1,), (1,)), ((), ()))
    centre_sq = jnp.sum(jnp.square(centres.astype(jnp.float32)), axis=1)
    stacked = slab.reshape(feat_count, rows_dev, feat_width)
    points = lax.all_to_all(stacked, "feat", split_axis=0, concat_axis=2, tiled=True)[0]
    cross_term = lax.dot_general(points, centres, contract, preferred_element_type=jnp.float32)
    point_sq = jnp.sum(jnp.square(points.astype(jnp.float32)), axis=1)
    nearest = jnp.min(point_sq[:, None] + centre_sq[None, :] - 2.0 * cross_term, axis=1)[None, :][0]
    member = labels[:, 0]
    cost_part = jax.ops.segment_sum(nearest, member, num_segments=centre_count)
    size_part = jax.ops.segment_sum(jnp.ones_like(nearest), member, num_segments=centre_count)
    cluster_cost, cluster_size = lax.psum((cost_part, size_part), ("pts", "feat"))
    own_sens = nearest / jnp.take(cluster_cost, member) + 1.0 / jnp.take(cluster_size, member)
    shard_sens = lax.all_gather(own_sens, "feat", axis=0, tiled=True)
    total_points = rows_pts * lax.axis_size("pts")
    weight = 2.0 * centre_count / total_points / shard_sens
    picked_rows = sample_rows[0]
    owner_count, slot_count = picked_rows.shape
    chosen = jnp.take(slab, picked_rows.reshape(-1), axis=0).reshape(
        owner_count, slot_count, feat_width
    )
    chosen_weight = jnp.take(weight, picked_rows)
    live_slot = jnp.arange(slot_count, dtype=jnp.int32)[None, :] < sample_count[0][:, None]
    scaled = jnp.where(
        live_slot[:, :, None], chosen.astype(jnp.float32) * chosen_weight[:, :, None], 0.0
    ).astype(jnp.bfloat16)
    arrived = lax.all_to_all(scaled, "pts", split_axis=0, concat_axis=0, tiled=True)
    target = slot_offset[0][:, None] + jnp.arange(slot_count, dtype=jnp.int32)[None, :]
    own_rows = arrived.shape[0] * slot_count
    placed = jnp.zeros((own_rows, feat_width), jnp.float32)
    placed = placed.at[target.reshape(-1)].add(
        arrived.reshape(-1, feat_width).astype(jnp.float32), mode="drop"
    )
    return placed.astype(jnp.bfloat16)


def solution(mesh):
    placed = (
        P("pts", "feat"),
        P(),
        P(("pts", "feat"), None),
        P("pts", None, None),
        P("pts", None),
        P("pts", None),
    )
    return jax.shard_map(
        local, mesh=mesh, in_specs=placed, out_specs=P("pts", "feat"), check_vma=False
    )
```

profile of v0, /device:TPU:0, one launch (start us, length us, event | category | flops | bytes accessed | tf_op | source)
XLA Modules:
  0.0 99.5 jit_solution(1397401444950790253)
XLA Ops:
  0.0 2.1 %copy.35 = bf16[24,4,8,512]{3,2,0,1:T(8,128)(2,1)} copy(bf16[24,4,8,512]{3,2,1,0:T(8,128)(2,1)} %bitcast.31) | data formatting | bytes 1572864 | tf_op jit(solution)/shard_map/reshape | solution.py:14
  2.1 4.2 %all-to-all-start = ((bf16[4,512,192]{1,2,0:T(8,128)(2,1)}), bf16[4,512,192]{1,2,0:T(8,128)(2,1)S(1)}, u32[]{:S(2)}, u32[]{:S(2)}) async-start(bf16[4,512,192]{1,2,0:T(8,128)(2,1)} %bitcast.29), calls=%async_computation | async-start | bytes 1572864 | tf_op jit(solution)/shard_map/all_to_all | solution.py:15
  6.3 1.4 %copy.28 = bf16[2048,192]{1,0:T(8,128)(2,1)S(1)} copy(bf16[2048,192]{0,1:T(8,128)(2,1)} %param.8) | data formatting | bytes 1572864 | tf_op args[0]
  7.8 0.7 compare_select_fusion.1
  8.4 0.8 copy.27
  9.2 0.7 compare_select_fusion
  9.9 0.1 copy.30
  10.0 0.1 reshape.185
  10.1 0.1 reshape_squeeze.6
  10.2 0.6 gather_fusion
  10.8 0.7 iota_compare_fusion
  11.5 0.7 iota_add_fusion
  12.3 0.1 add.119
  12.3 3.4 %scatter_custom_fusion.1 = f32[4096]{0:T(1024)S(1)} fusion(s32[512]{0:T(512)} %bitcast.35, f32[512]{0:T(512)S(1)} %broadcast.113, f32[]{:T(128)} %constant.22.clone.1), kind=kCustom, calls=%fused_computation.14 | custom fusion | flops 512 | bytes 16896 | tf_op jit(solution)/shard_map/scatter-add | solution.py:21
  15.8 4.1 %multiply_reduce_fusion = f32[4096]{0:T(1024)S(1)} fusion(bf16[4096,768]{1,0:T(8,128)(2,1)} %param.9), kind=kLoop, calls=%fused_computation.7 | loop fusion | flops 9433088 | bytes 6307840 | tf_op jit(solution)/shard_map/reduce_sum | solution.py:13
  19.8 0.0 all-to-all-done
  19.9 0.2 multiply_reduce_fusion.1
  20.1 0.0 copy-start.1
  20.1 7.5 %subtract_reduce_fusion = f32[512]{0:T(512)S(1)} fusion(bf16[512,768]{0,1:T(8,128)(2,1)S(1)} %bitcast.32, bf16[4096,768]{1,0:T(8,128)(2,1)} %param.9, f32[4096]{0:T(1024)S(1)} %multiply_reduce_fusion, f32[512]{0:T(512)S(1)} %multiply_reduce_fusion.1), kind=kOutput, calls=%fused_computation.8 | convolution fusion | flops 3229613568 | bytes 7098368 | tf_op jit(solution)/shard_map/dot_general | solution.py:16
  27.6 0.0 copy-done.1
  27.6 0.0 copy-start
  27.6 3.3 %scatter_custom_fusion = f32[4096]{0:T(1024)S(1)} fusion(s32[512]{0:T(512)S(1)} %bitcast.36, f32[512]{0:T(512)S(1)} %subtract_reduce_fusion, f32[]{:T(128)} %constant.22.clone.1), kind=kCustom, calls=%fused_computation.16 | custom fusion | flops 512 | bytes 16388 | tf_op jit(solution)/shard_map/scatter-add | solution.py:20
  30.9 42.0 %all-reduce = (f32[4096]{0:T(1024)S(1)}, f32[4096]{0:T(1024)S(1)}) all-reduce(f32[4096]{0:T(1024)S(1)} %scatter_custom_fusion.1, f32[4096]{0:T(1024)S(1)} %scatter_custom_fusion), channel_id=1, replica_groups=mesh['pts'=8,'feat'=4] {'pts','feat'}, use_global_device_ids=true, to_apply=%region_6.8 | all-reduce | flops 8192 | bytes 65536 | tf_op jit(solution)/shard_map/psum | solution.py:22
  72.9 3.1 %gather_fusion.2 = f32[512]{0:T(512)S(1)} fusion(f32[4096]{0:T(1024)S(1)} %get-tuple-element.7, s32[1024]{0:T(1024)S(1)} %pad_clamp_fusion.1), kind=kCustom, calls=%fused_computation.clone | custom fusion | bytes 6144 | tf_op jit(solution)/shard_map/jit(_take)/gather | solution.py:23
  76.0 3.1 %gather_fusion.3 = f32[512]{0:T(512)S(1)} fusion(f32[4096]{0:T(1024)S(1)} %get-tuple-element.6, s32[1024]{0:T(1024)S(1)} %pad_clamp_fusion.1), kind=kCustom, calls=%fused_computation.1.clone | custom fusion | bytes 6144 | tf_op jit(solution)/shard_map/jit(_take)/gather | solution.py:23
  79.2 5.5 %all-gather = f32[4,1,512]{2,1,0:T(1,128)S(1)} all-gather(f32[1,1,512]{2,1,0:T(1,128)S(1)} %bitcast.33), channel_id=1, replica_groups=mesh['pts'=8,'feat'=4] {'feat'}, dimensions={0}, use_global_device_ids=true | all-gather | bytes 10240 | tf_op jit(solution)/shard_map/all_gather | solution.py:24
  84.7 0.7 gather_fusion.1
  85.4 0.1 reshape.184
  85.4 0.1 copy.31
  85.5 0.0 copy-done
  85.5 0.1 copy.32
  85.6 0.1 copy.26
  85.7 0.7 select_convert_fusion
  86.4 5.1 %all-to-all-start.1 = ((bf16[8,4,192]{2,1,0:T(4,128)(2,1)}), bf16[8,4,192]{2,1,0:T(4,128)(2,1)S(1)}, u32[]{:S(2)}, u32[]{:S(2)}) async-start(bf16[8,4,192]{2,1,0:T(4,128)(2,1)} %select_convert_fusion), calls=%async_computation.1 | async-start | bytes 32768 | tf_op jit(solution)/shard_map/all_to_all | solution.py:37
  91.5 6.6 %all-to-all-done.1 = bf16[8,4,192]{2,1,0:T(4,128)(2,1)S(1)} async-done(((bf16[8,4,192]{2,1,0:T(4,128)(2,1)}), bf16[8,4,192]{2,1,0:T(4,128)(2,1)S(1)}, u32[]{:S(2)}, u32[]{:S(2)}) %all-to-all-start.1) | async-done | bytes 12320 | tf_op jit(solution)/shard_map/all_to_all | solution.py:37
  98.1 0.8 scatter_custom_fusion.2
  98.9 0.6 convert_element_type.28
  (11 shorter events, 0.1 us)
Async XLA Ops:
  2.1 17.8 %all-to-all-start = ((bf16[4,512,192]{1,2,0:T(8,128)(2,1)}), bf16[4,512,192]{1,2,0:T(8,128)(2,1)S(1)}, u32[]{:S(2)}, u32[]{:S(2)}) async-start(bf16[4,512,192]{1,2,0:T(8,128)(2,1)} %bitcast.29), calls=%async_computation | async-start | bytes 1572864 | tf_op jit(solution)/shard_map/all_to_all | solution.py:15
  20.1 7.5 %copy-start.1 = (s32[512,1]{0,1:T(1,128)S(1)}, s32[512,1]{0,1:T(1,128)}, u32[]{:S(2)}) copy-start(s32[512,1]{0,1:T(1,128)} %param.10) | copy-start | bytes 6148
  27.6 57.9 %copy-start = (s32[1,8,4]{1,2,0:T(4,128)S(1)}, s32[1,8,4]{1,2,0:T(4,128)}, u32[]{:S(2)}) copy-start(s32[1,8,4]{1,2,0:T(4,128)} %param.11) | copy-start | bytes 388
  86.4 11.6 %all-to-all-start.1 = ((bf16[8,4,192]{2,1,0:T(4,128)(2,1)}), bf16[8,4,192]{2,1,0:T(4,128)(2,1)S(1)}, u32[]{:S(2)}, u32[]{:S(2)}) async-start(bf16[8,4,192]{2,1,0:T(4,128)(2,1)} %select_convert_fusion), calls=%async_computation.1 | async-start | bytes 32768 | tf_op jit(solution)/shard_map/all_to_all | solution.py:37
where the time goes:
time: 100 us; the launch traced here: 99.5 us
  blocking collectives  47.4 us (47%)
  other arithmetic  15.9 us (16%)
  local copies, waits for them, and re-layouts  12.6 us (13%)
  starting transfers between devices  9.3 us (9%)
  matrix products  7.52 us (8%)
  waiting for transfers between devices  6.57 us (7%)
    psum x1, blocking collectives, local(): lax.psum((cost_part, size_part), ('pts', 'feat'))  42 us
    dot_general x1, matrix products, local(): lax.dot_general(points, centres, contract, preferred_element_type=jnp.flo...  7.52 us
    all_to_all x1, waiting for transfers between devices, local(): lax.all_to_all(scaled, 'pts', split_axis=0, concat_axis=0, tiled=True)  6.57 us
    all_gather x1, blocking collectives, local(): shard_sens = lax.all_gather(own_sens, 'feat', axis=0, tiled=True)  5.45 us
    all_to_all x1, starting transfers between devices, local(): lax.all_to_all(scaled, 'pts', split_axis=0, concat_axis=0, tiled=True)  5.07 us
    all_to_all x1, starting transfers between devices, local(): lax.all_to_all(stacked, 'feat', split_axis=0, concat_axis=2, tiled=True)[0]  4.24 us
    reduce_sum x1, other arithmetic, local(): centre_sq = jnp.sum(jnp.square(centres.astype(jnp.float32)), axis=1)  4.09 us
    scatter-add x1, other arithmetic, local(): jax.ops.segment_sum(jnp.ones_like(nearest), member, num_segments=centre_c...  3.39 us
  transfers between devices with their start and end apart: 2, of which 1 were waited for; matrix products, arithmetic and copies ran while one was open for 14% of the time, Pallas kernels for 0%

commit v1 on v0

--- a/solution.py
+++ b/solution.py
@@ -19,7 +19,7 @@
     member = labels[:, 0]
     cost_part = jax.ops.segment_sum(nearest, member, num_segments=centre_count)
     size_part = jax.ops.segment_sum(jnp.ones_like(nearest), member, num_segments=centre_count)
-    cluster_cost, cluster_size = lax.psum((cost_part, size_part), ("pts", "feat"))
+    cluster_cost, cluster_size = lax.psum(lax.psum((cost_part, size_part), "feat"), "pts")
     own_sens = nearest / jnp.take(cluster_cost, member) + 1.0 / jnp.take(cluster_size, member)
     shard_sens = lax.all_gather(own_sens, "feat", axis=0, tiled=True)
     total_points = rows_pts * lax.axis_size("pts")

time: 100 us -> 106 us (1.060)
  blocking collectives: 47.4 us -> 55.2 us
  starting transfers between devices: 9.3 us -> 7.57 us
    psum x1 -> x2, blocking collectives: 42 us -> 50 us  [the longest x1 37.9 us: local(): lax.psum(lax.psum((cost_part, size_part), 'feat'), 'pts')]
    all_to_all x1, starting transfers between devices: 5.07 us -> 3.34 us  [local(): lax.all_to_all(scaled, 'pts', split_axis=0, concat_axis=0, tiled=True)]
  transfers between devices with their start and end apart: 2 -> 2, of which waited for: 1 -> 1; matrix products, arithmetic and copies ran while one was open for 14% -> 13% of each run, Pallas kernels for 0% -> 0%
where the time goes in v1:
time: 106 us; the launch traced here: 105 us
  blocking collectives  55.2 us (52%)
  other arithmetic  15.9 us (15%)
  local copies, waits for them, and re-layouts  12.6 us (12%)
  starting transfers between devices  7.57 us (7%)
  matrix products  7.52 us (7%)
  waiting for transfers between devices  6.5 us (6%)
    psum x1, blocking collectives, local(): lax.psum(lax.psum((cost_part, size_part), 'feat'), 'pts')  37.9 us
    psum x1, blocking collectives, local(): lax.psum((cost_part, size_part), 'feat')  12.1 us
    dot_general x1, matrix products, local(): lax.dot_general(points, centres, contract, preferred_element_type=jnp.flo...  7.52 us
    all_to_all x1, waiting for transfers between devices, local(): lax.all_to_all(scaled, 'pts', split_axis=0, concat_axis=0, tiled=True)  6.5 us
    all_gather x1, blocking collectives, local(): shard_sens = lax.all_gather(own_sens, 'feat', axis=0, tiled=True)  5.19 us
    all_to_all x1, starting transfers between devices, local(): lax.all_to_all(stacked, 'feat', split_axis=0, concat_axis=2, tiled=True)[0]  4.24 us
    reduce_sum x1, other arithmetic, local(): centre_sq = jnp.sum(jnp.square(centres.astype(jnp.float32)), axis=1)  4.09 us
    scatter-add x1, other arithmetic, local(): jax.ops.segment_sum(jnp.ones_like(nearest), member, num_segments=centre_c...  3.39 us
  transfers between devices with their start and end apart: 2, of which 1 were waited for; matrix products, arithmetic and copies ran while one was open for 13% of the time, Pallas kernels for 0%

profile of v1, /device:TPU:0, one launch (start us, length us, event | category | flops | bytes accessed | tf_op | source)
XLA Modules:
  0.0 105.5 jit_solution(10556144194741030771)
XLA Ops:
  0.0 2.1 %copy.35 = bf16[24,4,8,512]{3,2,0,1:T(8,128)(2,1)} copy(bf16[24,4,8,512]{3,2,1,0:T(8,128)(2,1)} %bitcast.31) | data formatting | bytes 1572864 | tf_op jit(solution)/shard_map/reshape | solution.py:14
  2.1 4.2 %all-to-all-start = ((bf16[4,512,192]{1,2,0:T(8,128)(2,1)}), bf16[4,512,192]{1,2,0:T(8,128)(2,1)S(1)}, u32[]{:S(2)}, u32[]{:S(2)}) async-start(bf16[4,512,192]{1,2,0:T(8,128)(2,1)} %bitcast.29), calls=%async_computation | async-start | bytes 1572864 | tf_op jit(solution)/shard_map/all_to_all | solution.py:15
  6.3 1.4 %copy.28 = bf16[2048,192]{1,0:T(8,128)(2,1)S(1)} copy(bf16[2048,192]{0,1:T(8,128)(2,1)} %param.8) | data formatting | bytes 1572864 | tf_op args[0]
  7.8 0.7 compare_select_fusion.1
  8.4 0.8 copy.27
  9.2 0.7 compare_select_fusion
  9.9 0.1 copy.30
  10.0 0.1 reshape.185
  10.1 0.1 reshape_squeeze.6
  10.2 0.6 gather_fusion
  10.8 0.7 iota_compare_fusion
  11.5 0.7 iota_add_fusion
  12.3 0.1 add.123
  12.3 3.4 %scatter_custom_fusion.1 = f32[4096]{0:T(1024)S(1)} fusion(s32[512]{0:T(512)} %bitcast.35, f32[512]{0:T(512)S(1)} %broadcast.113, f32[]{:T(128)} %constant.22.clone.1), kind=kCustom, calls=%fused_computation.14 | custom fusion | flops 512 | bytes 16896 | tf_op jit(solution)/shard_map/scatter-add | solution.py:21
  15.8 4.1 %multiply_reduce_fusion = f32[4096]{0:T(1024)S(1)} fusion(bf16[4096,768]{1,0:T(8,128)(2,1)} %param.9), kind=kLoop, calls=%fused_computation.7 | loop fusion | flops 9433088 | bytes 6307840 | tf_op jit(solution)/shard_map/reduce_sum | solution.py:13
  19.8 0.0 all-to-all-done
  19.9 0.2 multiply_reduce_fusion.1
  20.1 0.0 copy-start.1
  20.1 7.5 %subtract_reduce_fusion = f32[512]{0:T(512)S(1)} fusion(bf16[512,768]{0,1:T(8,128)(2,1)S(1)} %bitcast.32, bf16[4096,768]{1,0:T(8,128)(2,1)} %param.9, f32[4096]{0:T(1024)S(1)} %multiply_reduce_fusion, f32[512]{0:T(512)S(1)} %multiply_reduce_fusion.1), kind=kOutput, calls=%fused_computation.8 | convolution fusion | flops 3229613568 | bytes 7098368 | tf_op jit(solution)/shard_map/dot_general | solution.py:16
  27.6 0.0 copy-done.1
  27.6 0.0 copy-start
  27.6 3.3 %scatter_custom_fusion = f32[4096]{0:T(1024)S(1)} fusion(s32[512]{0:T(512)S(1)} %bitcast.36, f32[512]{0:T(512)S(1)} %subtract_reduce_fusion, f32[]{:T(128)} %constant.22.clone.1), kind=kCustom, calls=%fused_computation.16 | custom fusion | flops 512 | bytes 16388 | tf_op jit(solution)/shard_map/scatter-add | solution.py:20
  30.9 12.1 %all-reduce.1 = (f32[4096]{0:T(1024)S(1)}, f32[4096]{0:T(1024)S(1)}) all-reduce(f32[4096]{0:T(1024)S(1)} %scatter_custom_fusion.1, f32[4096]{0:T(1024)S(1)} %scatter_custom_fusion), channel_id=1, replica_groups=mesh['pts'=8,'feat'=4] {'feat'}, use_global_device_ids=true, to_apply=%region_7.9 | all-reduce | flops 8192 | bytes 65536 | tf_op jit(solution)/shard_map/psum | solution.py:22
  43.0 37.9 %all-reduce = (f32[4096]{0:T(1024)S(1)}, f32[4096]{0:T(1024)S(1)}) all-reduce(f32[4096]{0:T(1024)S(1)} %get-tuple-element.8, f32[4096]{0:T(1024)S(1)} %get-tuple-element.9), channel_id=1, replica_groups=mesh['pts'=8,'feat'=4] {'pts'}, use_global_device_ids=true, to_apply=%region_8.10 | all-reduce | flops 8192 | bytes 65536 | tf_op jit(solution)/shard_map/psum | solution.py:22
  80.9 3.1 %gather_fusion.2 = f32[512]{0:T(512)S(1)} fusion(f32[4096]{0:T(1024)S(1)} %get-tuple-element.7, s32[1024]{0:T(1024)S(1)} %pad_clamp_fusion.1), kind=kCustom, calls=%fused_computation.clone | custom fusion | bytes 6144 | tf_op jit(solution)/shard_map/jit(_take)/gather | solution.py:23
  84.1 3.1 %gather_fusion.3 = f32[512]{0:T(512)S(1)} fusion(f32[4096]{0:T(1024)S(1)} %get-tuple-element.6, s32[1024]{0:T(1024)S(1)} %pad_clamp_fusion.1), kind=kCustom, calls=%fused_computation.1.clone | custom fusion | bytes 6144 | tf_op jit(solution)/shard_map/jit(_take)/gather | solution.py:23
  87.2 5.2 %all-gather = f32[4,1,512]{2,1,0:T(1,128)S(1)} all-gather(f32[1,1,512]{2,1,0:T(1,128)S(1)} %bitcast.33), channel_id=1, replica_groups=mesh['pts'=8,'feat'=4] {'feat'}, dimensions={0}, use_global_device_ids=true | all-gather | bytes 10240 | tf_op jit(solution)/shard_map/all_gather | solution.py:24
  92.4 0.7 gather_fusion.1
  93.1 0.1 reshape.184
  93.2 0.1 copy.31
  93.3 0.0 copy-done
  93.3 0.1 copy.32
  93.4 0.1 copy.26
  93.5 0.7 select_convert_fusion
  94.2 3.3 %all-to-all-start.1 = ((bf16[8,4,192]{2,1,0:T(4,128)(2,1)}), bf16[8,4,192]{2,1,0:T(4,128)(2,1)S(1)}, u32[]{:S(2)}, u32[]{:S(2)}) async-start(bf16[8,4,192]{2,1,0:T(4,128)(2,1)} %select_convert_fusion), calls=%async_computation.1 | async-start | bytes 32768 | tf_op jit(solution)/shard_map/all_to_all | solution.py:37
  97.6 6.5 %all-to-all-done.1 = bf16[8,4,192]{2,1,0:T(4,128)(2,1)S(1)} async-done(((bf16[8,4,192]{2,1,0:T(4,128)(2,1)}), bf16[8,4,192]{2,1,0:T(4,128)(2,1)S(1)}, u32[]{:S(2)}, u32[]{:S(2)}) %all-to-all-start.1) | async-done | bytes 12320 | tf_op jit(solution)/shard_map/all_to_all | solution.py:37
  104.1 0.8 scatter_custom_fusion.2
  104.9 0.6 convert_element_type.28
  (11 shorter events, 0.1 us)
Async XLA Ops:
  2.1 17.8 %all-to-all-start = ((bf16[4,512,192]{1,2,0:T(8,128)(2,1)}), bf16[4,512,192]{1,2,0:T(8,128)(2,1)S(1)}, u32[]{:S(2)}, u32[]{:S(2)}) async-start(bf16[4,512,192]{1,2,0:T(8,128)(2,1)} %bitcast.29), calls=%async_computation | async-start | bytes 1572864 | tf_op jit(solution)/shard_map/all_to_all | solution.py:15
  20.1 7.5 %copy-start.1 = (s32[512,1]{0,1:T(1,128)S(1)}, s32[512,1]{0,1:T(1,128)}, u32[]{:S(2)}) copy-start(s32[512,1]{0,1:T(1,128)} %param.10) | copy-start | bytes 6148
  27.6 65.7 %copy-start = (s32[1,8,4]{1,2,0:T(4,128)S(1)}, s32[1,8,4]{1,2,0:T(4,128)}, u32[]{:S(2)}) copy-start(s32[1,8,4]{1,2,0:T(4,128)} %param.11) | copy-start | bytes 388
  94.2 9.9 %all-to-all-start.1 = ((bf16[8,4,192]{2,1,0:T(4,128)(2,1)}), bf16[8,4,192]{2,1,0:T(4,128)(2,1)S(1)}, u32[]{:S(2)}, u32[]{:S(2)}) async-start(bf16[8,4,192]{2,1,0:T(4,128)(2,1)} %select_convert_fusion), calls=%async_computation.1 | async-start | bytes 32768 | tf_op jit(solution)/shard_map/all_to_all | solution.py:37
